TPU v7x, 512 devices: a whole 4x8x8 slice. The times are simulated.
512 devices in a mesh: grp: 64 (over x, y, core), swap: 8 (over z).
Axes of the slice: x: 4, y: 8, z: 8, core: 2. Of those that a mesh axis runs over, the one named last changes fastest.
Arguments:
- samples: bfloat16 [8, 64, 64, 4, 4096], P('swap', 'grp'), may hold values from 0.049804688 to 4
- tile_list: int32 [8, 64, 64], replicated, may hold values from 0 to 511, as said below
- tile_slot: int32 [512], replicated, may hold values from 0 to 511, as said below
- brick_rank: int32 [8, 512], replicated, may hold values from 0 to 511, each once within a row
Outputs:
- final_image: float32 [64, 8, 4, 4096], P('grp', None, None, 'swap')
Inputs may be any that keep to these rules, and one draw needn't show every extreme that they name: `tile_list`: the 64 tiles of one device are distinct; fragments b * 8 to (b + 1) * 8 - 1 of a device belong to its brick b. With owner(t) = tile_slot[t] // 8, each device has 2 tiles of each of a quarter of the owners of its group, 1 of each of half of them and none of the rest; in every slab one owner has 2 tiles from every device of the group. A permutation: tile t is row tile_slot[t] % 8 of owner tile_slot[t] // 8.
All inputs are finite; a program needn't handle non-finite values.
Results may differ from a plain program's by a relative error of at most 0.0003.
Values sent between devices are 32-bit elements; how exact they have to be, the bound alone decides.
A program may use at most 64 MiB of HBM per device.

v0:
```python
import jax
import jax.numpy as jnp
from jax import lax
from jax.sharding import PartitionSpec as P

BRICKS = 8


EXTINCTION = 0.024


def from_partner(array, axis, apart):
    return lax.ppermute(array, axis, [(i, i ^ 1 << apart) for i in range(lax.axis_size(axis))])


def render(values_in):
    depth_count = values_in.shape[1]
    shape = (values_in.shape[0], values_in.shape[2])
    before = jnp.zeros(shape, jnp.float32)
    red_sum = jnp.zeros(shape, jnp.float32)
    green_sum = jnp.zeros(shape, jnp.float32)
    blue_sum = jnp.zeros(shape, jnp.float32)
    for level in range(depth_count):
        values = values_in[:, level].astype(jnp.float32)
        extinction = EXTINCTION * values
        weight = jnp.exp(-before) * (1.0 - jnp.exp(-extinction))
        ratio = values / (1.0 + values)
        red_sum = red_sum + weight * ratio
        green_sum = green_sum + weight * 4.0 * ratio * (1.0 - ratio)
        blue_sum = blue_sum + weight * (1.0 - ratio)
        before = before + extinction
    return jnp.stack([red_sum, green_sum, blue_sum, before], axis=1)


def over_pair(front_part, back_part):
    colors = front_part[:, :3] + jnp.exp(-front_part[:, 3:4]) * back_part[:, :3]
    return jnp.concatenate([colors, front_part[:, 3:4] + back_part[:, 3:4]], axis=1)


def slot_tables(tiles_in, tile_slot, owned, per_brick, ranks_in):
    group_count, per_device = tiles_in.shape
    slot_ids = tile_slot[tiles_in]
    owners = slot_ids // owned
    tile_rows = slot_ids % owned
    position = jnp.arange(per_device, dtype=jnp.int32)
    same_owner = (owners[:, :, None] == owners[:, None, :]) & (
        position[None, None, :] < position[None, :, None]
    )
    places = jnp.sum(same_owner.astype(jnp.int32), axis=2)
    depth_keys = jnp.repeat(ranks_in.reshape(group_count, BRICKS), per_brick, axis=1)
    return (owners, tile_rows, places, depth_keys)


def arrivals(owners, tile_rows, places, depth_keys, device, capacity):
    slot_ids = jnp.arange(capacity, dtype=jnp.int32)
    matched = (
        (owners[:, None, :] == device) & (places[:, None, :] == slot_ids[None, :, None])
    ).astype(jnp.int32)
    rows_in = jnp.sum(matched * tile_rows[:, None, :], axis=2).reshape(-1)
    keys_in = jnp.sum(matched * depth_keys[:, None, :], axis=2).reshape(-1)
    valid_in = (jnp.sum(matched, axis=2) > 0).reshape(-1)
    return (rows_in, keys_in, valid_in)


def outgoing(fragments, owners_mine, places_mine, group_count, capacity):
    per_device = fragments.shape[0]
    target = owners_mine * capacity + places_mine
    slot_ids = jnp.arange(group_count * capacity, dtype=jnp.int32)
    matched = (target[None, :] == slot_ids[:, None]).astype(jnp.int32)
    numbers = jnp.arange(per_device, dtype=jnp.int32) + 1
    source = jnp.sum(matched * numbers[None, :], axis=1) - 1
    source = jnp.where(source < 0, per_device, source)
    padded = jnp.concatenate(
        [fragments, jnp.zeros((1,) + fragments.shape[1:], jnp.float32)], axis=0
    )
    return jnp.take(padded, source, axis=0)


def combine(pieces, rows_in, keys_in, valid_in, owned):
    optical = pieces[:, 3]
    both_valid = valid_in[:, None] & valid_in[None, :]
    in_front = (
        (rows_in[:, None] == rows_in[None, :]) & both_valid & (keys_in[None, :] < keys_in[:, None])
    ).astype(jnp.float32)
    prefix = jnp.dot(
        in_front, optical, precision=lax.Precision.HIGHEST, preferred_element_type=jnp.float32
    )
    shaded = pieces[:, :3] * jnp.exp(-prefix)[:, None]
    to_rows = (
        (jnp.arange(owned, dtype=jnp.int32)[:, None] == rows_in[None, :]) & valid_in[None, :]
    ).astype(jnp.float32)
    colors = jnp.einsum("of,fcp->ocp", to_rows, shaded, precision=lax.Precision.HIGHEST)
    summed = jnp.dot(
        to_rows, optical, precision=lax.Precision.HIGHEST, preferred_element_type=jnp.float32
    )
    return jnp.concatenate([colors, summed[:, None]], axis=1)


def leaving_of(fragments, owners_slab, places_slab, device, group_count, capacity):
    owners_mine = lax.dynamic_index_in_dim(owners_slab, device, 0, keepdims=False)
    places_mine = lax.dynamic_index_in_dim(places_slab, device, 0, keepdims=False)
    return outgoing(fragments, owners_mine, places_mine, group_count, capacity)


def shards(samples, tile_list, tile_slot, brick_rank):
    group_count = lax.axis_size("grp")
    swap_count = lax.axis_size("swap")
    device = lax.axis_index("grp")
    slab = lax.axis_index("swap")
    per_device = tile_list.shape[2]
    per_brick = per_device // BRICKS
    owned = tile_slot.shape[0] // group_count
    capacity = 2 * per_device // group_count
    pixels = samples.shape[4]
    block = pixels // swap_count
    fragments = render(samples[0, 0])
    tiles_slab = lax.dynamic_index_in_dim(tile_list, slab, 0, keepdims=False)
    ranks_slab = lax.dynamic_index_in_dim(brick_rank, slab, 0, keepdims=False)
    owners_slab, rows_slab, places_slab, keys_slab = slot_tables(
        tiles_slab, tile_slot, owned, per_brick, ranks_slab
    )
    leaving = leaving_of(fragments, owners_slab, places_slab, device, group_count, capacity)
    rows_in, keys_in, valid_in = arrivals(
        owners_slab, rows_slab, places_slab, keys_slab, device, capacity
    )
    arrived = lax.all_to_all(
        leaving.reshape(group_count, capacity, 4, pixels),
        "grp",
        split_axis=0,
        concat_axis=0,
        tiled=True,
    )
    partial_value = combine(
        arrived.reshape(-1, 4, arrived.shape[3]), rows_in, keys_in, valid_in, owned
    )
    levels = swap_count.bit_length() - 1
    partial_value = partial_value.reshape((owned, 4) + (2,) * levels + (block,))
    for level in range(levels):
        lower = partial_value[..., 0, :]
        upper = partial_value[..., 1, :]
        my_bit = jnp.right_shift(slab, level) % 2
        kept = jnp.where(my_bit == 1, upper, lower)
        given = jnp.where(my_bit == 1, lower, upper)
        received = from_partner(given, "swap", level)
        front_part = jnp.where(my_bit == 0, kept, received)
        back_part = jnp.where(my_bit == 0, received, kept)
        partial_value = over_pair(front_part, back_part)
    final_image = jnp.concatenate(
        [partial_value[:, :3], 1.0 - jnp.exp(-partial_value[:, 3:4])], axis=1
    )
    return final_image[None]


def solution(mesh):
    return jax.shard_map(
        shards,
        mesh=mesh,
        in_specs=(P("swap", "grp", None, None, None), P(), P(), P()),
        out_specs=P("grp", None, None, "swap"),
        check_vma=False,
    )
```

profile of v0, /device:TPU:1, one launch (start us, length us, event | category | flops | bytes accessed | tf_op | source)
XLA Modules:
  0.0 315.6 jit_solution(5608648310133044078)
XLA Ops:
  0.0 0.8 compare_select_fusion
  0.9 25.9 %gather_fusion = s32[4096]{0:T(1024)S(1)} fusion(s32[512]{0:T(512)S(1)} %copy-done.1, s32[4096]{0:T(1024)S(1)} %broadcast_clamp_fusion), kind=kCustom, calls=%fused_computation | custom fusion | bytes 49152 | tf_op jit(solution)/shard_map/gather | solution.py:42
  26.9 1.9 convert_reduce_fusion
  29.2 0.1 sub.70
  29.4 0.2 select_reduce_fusion
  29.7 0.1 copy.43
  29.8 1.2 copy.70
  31.0 2.7 fusion.31
  33.7 0.3 pad_maximum_fusion
  34.0 2.7 copy.59
  36.7 2.8 concatenate.18.clone
  39.5 11.5 %gather_fusion.1 = f32[128,4,4096]{2,1,0:T(4,128)} fusion(f32[65,4,4096]{2,1,0:T(4,128)} %concatenate.18.clone, s32[1024]{0:T(1024)S(1)} %pad_clamp_fusion), kind=kCustom, calls=%fused_computation.1 | custom fusion | bytes 16777728 | tf_op jit(solution)/shard_map/jit(_take)/gather | solution.py:76
  51.0 10.6 %broadcast_select_fusion = f32[64,2,4,4096]{3,2,1,0:T(4,128)} fusion(f32[64,2,4,4096]{3,2,1,0:T(4,128)} %bitcast.59, pred[64,2]{1,0:T(8,128)(4,1)S(1)} %copy.43), kind=kLoop, calls=%fused_computation.7 | loop fusion | flops 2097152 | bytes 16777344 | tf_op jit(solution)/shard_map/jit(_take)/select_n | solution.py:76
  61.5 11.9 %all-to-all-start = ((f32[64,2,4,4096]{3,2,1,0:T(4,128)}), f32[64,2,4,4096]{3,2,1,0:T(4,128)}, u32[]{:S(2)}, u32[]{:S(2)}) async-start(f32[64,2,4,4096]{3,2,1,0:T(4,128)} %broadcast_select_fusion), calls=%async_computation | async-start | bytes 16777216 | tf_op jit(solution)/shard_map/all_to_all | solution.py:126
  73.6 0.1 gt.19
  73.9 0.1 eq.125
  74.1 0.1 lt.129
  74.3 185.0 %all-to-all-done = f32[64,2,4,4096]{3,2,1,0:T(4,128)} async-done(((f32[64,2,4,4096]{3,2,1,0:T(4,128)}), f32[64,2,4,4096]{3,2,1,0:T(4,128)}, u32[]{:S(2)}, u32[]{:S(2)}) %all-to-all-start) | async-done | bytes 8388640 | tf_op jit(solution)/shard_map/all_to_all | solution.py:126
  259.3 5.7 %slice.108 = f32[128,1,4096]{2,1,0:T(1,128)S(1)} slice(f32[128,4,4096]{2,1,0:T(4,128)} %bitcast.7), slice={[0:128], [3:4], [0:4096]} | slice | bytes 4194304 | tf_op jit(solution)/shard_map/slice | solution.py:80
  264.9 3.9 %copy.60 = f32[128,1,4096]{0,2,1:T(8,128)} copy(f32[128,1,4096]{2,1,0:T(1,128)S(1)} %slice.108) | data formatting | bytes 4194304 | tf_op jit(solution)/shard_map/dot_general | solution.py:93
  268.8 2.6 fusion.1
  271.5 8.9 %fusion = f32[8,3,4096]{2,0,1:T(8,128)S(1)} fusion(f32[128,3,4096]{2,1,0:T(4,128)} %bitcast.58, f32[128,4096]{1,0:T(8,128)S(1)} %fusion.1, s32[128]{0:T(128)S(1)} %eq.125, pred[128]{0:T(512)(128)(4,1)S(1)} %gt.19), kind=kOutput, calls=%fused_computation.3 | convolution fusion | flops 152569856 | bytes 8782464 | tf_op jit(solution)/shard_map/of,fcp->ocp/dot_general | solution.py:92
  280.4 0.3 concatenate.19
  280.7 0.2 copy.52
  281.0 1.1 fusion.12
  282.1 3.8 %collective-permute-start = (f32[8,4,2,2,512]{4,0,1,2,3:T(8,128)S(1)}, f32[8,4,2,2,512]{4,0,1,2,3:T(8,128)S(1)}, u32[]{:S(2)}, u32[]{:S(2)}) collective-permute-start(f32[8,4,2,2,512]{4,0,1,2,3:T(8,128)S(1)} %select_bitcast_fusion), channel_id=1, source_target_pairs={{0,1},{1,0},{2,3},{3,2},{4,5},{5,4},{6,7},{7,6},{8,9},{9,8},{10,11... | collective-permute-start | bytes 786440 | tf_op jit(solution)/shard_map/ppermute | solution.py:13
  285.9 6.3 %collective-permute-done = f32[8,4,2,2,512]{4,0,1,2,3:T(8,128)S(1)} collective-permute-done((f32[8,4,2,2,512]{4,0,1,2,3:T(8,128)S(1)}, f32[8,4,2,2,512]{4,0,1,2,3:T(8,128)S(1)}, u32[]{:S(2)}, u32[]{:S(2)}) %collective-permute-start) | collective-permute-done | bytes 262176 | tf_op jit(solution)/shard_map/ppermute | solution.py:13
  292.4 5.8 %collective-permute-start.1 = (f32[8,4,2,512]{3,0,1,2:T(8,128)S(1)}, f32[8,4,2,512]{3,0,1,2:T(8,128)S(1)}, u32[]{:S(2)}, u32[]{:S(2)}) collective-permute-start(f32[8,4,2,512]{3,0,1,2:T(8,128)S(1)} %select_bitcast_fusion.1), channel_id=1, source_target_pairs={{0,2},{1,3},{2,0},{3,1},{4,6},{5,7},{6,4},{7,5},{8,10},{9,11},{10,... | collective-permute-start | bytes 393224 | tf_op jit(solution)/shard_map/ppermute | solution.py:13
  298.2 6.3 %collective-permute-done.1 = f32[8,4,2,512]{3,0,1,2:T(8,128)S(1)} collective-permute-done((f32[8,4,2,512]{3,0,1,2:T(8,128)S(1)}, f32[8,4,2,512]{3,0,1,2:T(8,128)S(1)}, u32[]{:S(2)}, u32[]{:S(2)}) %collective-permute-start.1) | collective-permute-done | bytes 131104 | tf_op jit(solution)/shard_map/ppermute | solution.py:13
  304.6 8.6 %collective-permute-start.2 = (f32[8,4,512]{2,0,1:T(8,128)S(1)}, f32[8,4,512]{2,0,1:T(8,128)S(1)}, u32[]{:S(2)}, u32[]{:S(2)}) collective-permute-start(f32[8,4,512]{2,0,1:T(8,128)S(1)} %select_bitcast_fusion.2), channel_id=1, source_target_pairs={{0,4},{1,5},{2,6},{3,7},{4,0},{5,1},{6,2},{7,3},{8,12},{9,13},{10,... | collective-permute-start | bytes 196616 | tf_op jit(solution)/shard_map/ppermute | solution.py:13
  313.2 1.6 collective-permute-done.2
  314.9 0.7 copy.53
  (43 shorter events, 1.3 us)
Async XLA Ops:
  0.0 28.9 %copy-start = (s32[8,512]{1,0:T(8,128)S(1)}, s32[8,512]{1,0:T(8,128)}, u32[]{:S(2)}) copy-start(s32[8,512]{1,0:T(8,128)} %param.7) | copy-start | bytes 49156
  0.0 0.9 copy-start.1
  0.9 28.9 %copy-start.3 = (bf16[1,1,64,4,4096]{4,3,2,1,0:T(4,128)(2,1)S(1)}, bf16[1,1,64,4,4096]{4,3,2,1,0:T(4,128)(2,1)}, u32[]{:S(2)}) copy-start(bf16[1,1,64,4,4096]{4,3,2,1,0:T(4,128)(2,1)} %param.4) | copy-start | bytes 6291460
  61.5 197.7 %all-to-all-start = ((f32[64,2,4,4096]{3,2,1,0:T(4,128)}), f32[64,2,4,4096]{3,2,1,0:T(4,128)}, u32[]{:S(2)}, u32[]{:S(2)}) async-start(f32[64,2,4,4096]{3,2,1,0:T(4,128)} %broadcast_select_fusion), calls=%async_computation | async-start | bytes 16777216 | tf_op jit(solution)/shard_map/all_to_all | solution.py:126
  271.4 9.5 %copy-start.2 = (f32[128,1,4096]{0,2,1:T(8,128)S(1)}, f32[128,1,4096]{0,2,1:T(8,128)}, u32[]{:S(2)}) copy-start(f32[128,1,4096]{0,2,1:T(8,128)} %copy.60) | copy-start | bytes 6291460
  282.1 10.2 %collective-permute-start = (f32[8,4,2,2,512]{4,0,1,2,3:T(8,128)S(1)}, f32[8,4,2,2,512]{4,0,1,2,3:T(8,128)S(1)}, u32[]{:S(2)}, u32[]{:S(2)}) collective-permute-start(f32[8,4,2,2,512]{4,0,1,2,3:T(8,128)S(1)} %select_bitcast_fusion), channel_id=1, source_target_pairs={{0,1},{1,0},{2,3},{3,2},{4,5},{5,4},{6,7},{7,6},{8,9},{9,8},{10,11... | collective-permute-start | bytes 786440 | tf_op jit(solution)/shard_map/ppermute | solution.py:13
  292.4 12.1 %collective-permute-start.1 = (f32[8,4,2,512]{3,0,1,2:T(8,128)S(1)}, f32[8,4,2,512]{3,0,1,2:T(8,128)S(1)}, u32[]{:S(2)}, u32[]{:S(2)}) collective-permute-start(f32[8,4,2,512]{3,0,1,2:T(8,128)S(1)} %select_bitcast_fusion.1), channel_id=1, source_target_pairs={{0,2},{1,3},{2,0},{3,1},{4,6},{5,7},{6,4},{7,5},{8,10},{9,11},{10,... | collective-permute-start | bytes 393224 | tf_op jit(solution)/shard_map/ppermute | solution.py:13
  304.6 10.3 %collective-permute-start.2 = (f32[8,4,512]{2,0,1:T(8,128)S(1)}, f32[8,4,512]{2,0,1:T(8,128)S(1)}, u32[]{:S(2)}, u32[]{:S(2)}) collective-permute-start(f32[8,4,512]{2,0,1:T(8,128)S(1)} %select_bitcast_fusion.2), channel_id=1, source_target_pairs={{0,4},{1,5},{2,6},{3,7},{4,0},{5,1},{6,2},{7,3},{8,12},{9,13},{10,... | collective-permute-start | bytes 196616 | tf_op jit(solution)/shard_map/ppermute | solution.py:13
where the time goes:
time: 316 us
  waiting for transfers between devices  199 us (63%)
  local copies, waits for them, and re-layouts  56.3 us (18%)
  starting transfers between devices  30.2 us (10%)
  other arithmetic  16.9 us (5%)
  matrix products  12.6 us (4%)
    all_to_all x1, waiting for transfers between devices, shards(): lax.all_to_all(leaving.reshape(group_count, capacity, 4, pixels), 'grp',...  185 us
    gather x2, local copies, waits for them, and re-layouts, slot_tables(): slot_ids = tile_slot[tiles_in]  26 us
    ppermute x3, starting transfers between devices, from_partner(): lax.ppermute(array, axis, [(i, i ^ 1 << apart) for i in range(lax.axis_si...  18.2 us
    ppermute x3, waiting for transfers between devices, from_partner(): lax.ppermute(array, axis, [(i, i ^ 1 << apart) for i in range(lax.axis_si...  14.2 us
    all_to_all x1, starting transfers between devices, shards(): lax.all_to_all(leaving.reshape(group_count, capacity, 4, pixels), 'grp',...  11.9 us
    gather x1, local copies, waits for them, and re-layouts, outgoing(): return jnp.take(padded, source, axis=0)  11.5 us
    select_n x2, other arithmetic, outgoing(): return jnp.take(padded, source, axis=0)  10.6 us
    dot_general x1, matrix products, combine(): jnp.einsum('of,fcp->ocp', to_rows, shaded, precision=lax.Precision.HIGHEST)  8.91 us
  transfers between devices with their start and end apart: 4, of which 4 were waited for; matrix products, arithmetic and copies ran while one was open for 0% of the time, Pallas kernels for 0%

commit v1 on v0

v1 whole, which is shorter than its diff:
```python
import jax
import jax.numpy as jnp
from jax import lax
from jax.experimental import pallas as pl
from jax.experimental.pallas import tpu as pltpu
from jax.sharding import PartitionSpec as P

BRICKS = 8
LANES = 128
HALF = 64

EXTINCTION = 0.024


def halves(shape):
    return lax.broadcasted_iota(jnp.int32, shape, len(shape) - 1) < HALF


def swapped(value):
    return pltpu.roll(value, HALF, value.ndim - 1)


def render_kernel(samples_ref, out_ref, levels):
    fragments, depth_count, width = samples_ref.shape
    low = halves((fragments, LANES))
    low_half = halves((fragments // 2, LANES))
    for row in range(width // LANES):
        values = samples_ref[:, :, row * LANES : (row + 1) * LANES].astype(jnp.float32)
        levels[...] = values
        passed = jnp.ones((fragments, LANES), jnp.float32)
        red = jnp.zeros((fragments, LANES), jnp.float32)
        green = jnp.zeros((fragments, LANES), jnp.float32)
        for level in range(depth_count):
            value = levels[:, level, :]
            through = jnp.exp(-EXTINCTION * value)
            weight = passed * (1.0 - through)
            rest = 1.0 / (1.0 + value)
            ratio = value * rest
            shade = weight * ratio
            red = red + shade
            green = green + shade * 4.0 * rest
            passed = passed * through
        red_swapped, green_swapped, passed_swapped = swapped(red), swapped(green), swapped(passed)
        half = fragments // 2
        out_ref[2 * row, :fragments, :] = jnp.where(low, red, green_swapped)
        out_ref[2 * row + 1, :fragments, :] = jnp.where(low, red_swapped, green)
        out_ref[2 * row, fragments:, :] = jnp.where(low_half, passed[:half], passed_swapped[half:])
        out_ref[2 * row + 1, fragments:, :] = jnp.where(
            low_half, passed_swapped[:half], passed[half:]
        )


def render(samples, group_count):
    fragments, depth_count, pixels = samples.shape
    steps = 8
    width = pixels // steps
    rows = fragments + fragments // 2
    return pl.pallas_call(
        render_kernel,
        grid=(steps,),
        in_specs=[pl.BlockSpec((fragments, depth_count, width), lambda i: (0, 0, i))],
        out_specs=pl.BlockSpec((group_count // steps, rows, LANES), lambda i: (i, 0, 0)),
        out_shape=jax.ShapeDtypeStruct((group_count, rows, LANES), jnp.float32),
        scratch_shapes=[pltpu.VMEM((fragments, depth_count, LANES), jnp.float32)],
    )(samples)


def composite_kernel(order_ref, slots_ref, pieces_ref, out_ref, through, colors, passed):
    sources, rows, _ = pieces_ref.shape
    fragments = rows * 2 // 3
    half = fragments // 2
    per_brick = fragments // BRICKS
    low_half = halves((half, LANES))

    def widen(source, carry):
        packed = pieces_ref[source, fragments:, :]
        turned = swapped(packed)
        at = pl.multiple_of(source * fragments, fragments)
        through[pl.ds(at, half), :] = jnp.where(low_half, packed, turned)
        through[pl.ds(at + half, half), :] = jnp.where(low_half, turned, packed)
        return carry

    lax.fori_loop(0, sources, widen, 0)
    colors[...] = jnp.zeros_like(colors)
    passed[...] = jnp.ones_like(passed)

    def brick_step(rank, carry):
        brick = order_ref[rank]
        source = brick // BRICKS
        first = (brick % BRICKS) * per_brick
        number = brick * per_brick
        slots = [slots_ref[number + i] for i in range(per_brick)]
        seen = [passed[pl.ds(slot, 1), :] for slot in slots]
        held = [colors[pl.ds(slot, 1), :] for slot in slots]
        shades = [pieces_ref[source, pl.ds(first + i, 1), :] for i in range(per_brick)]
        fades = [through[pl.ds(number + i, 1), :] for i in range(per_brick)]
        for i in range(per_brick):
            colors[pl.ds(slots[i], 1), :] = held[i] + seen[i] * shades[i]
            passed[pl.ds(slots[i], 1), :] = seen[i] * fades[i]
        return carry

    lax.fori_loop(0, order_ref.shape[0], brick_step, 0)
    owned = out_ref.shape[1] // 2
    for owner in range(out_ref.shape[0]):
        out_ref[owner, :owned, :] = colors[owner * owned : (owner + 1) * owned, :]
        out_ref[owner, owned:, :] = passed[owner * owned : (owner + 1) * owned, :]


def composite(pieces, order, slots, owned):
    sources, rows, _ = pieces.shape
    fragments = rows * 2 // 3
    screen = sources * owned
    return pl.pallas_call(
        composite_kernel,
        in_specs=[
            pl.BlockSpec(memory_space=pltpu.SMEM),
            pl.BlockSpec(memory_space=pltpu.SMEM),
            pl.BlockSpec(memory_space=pltpu.VMEM),
        ],
        out_specs=pl.BlockSpec(memory_space=pltpu.VMEM),
        out_shape=jax.ShapeDtypeStruct((sources, 2 * owned, LANES), jnp.float32),
        scratch_shapes=[
            pltpu.VMEM((sources * fragments, LANES), jnp.float32),
            pltpu.VMEM((screen, LANES), jnp.float32),
            pltpu.VMEM((screen, LANES), jnp.float32),
        ],
    )(order, slots, pieces)


def finish_kernel(parts_ref, out_ref):
    slabs, blocks, rows, _ = parts_ref.shape
    owned = rows // 2
    low = halves((owned, LANES))
    for pair in range(blocks // 2):
        ends = []
        for side in range(2):
            block = 2 * pair + side
            color = parts_ref[0, block, :owned, :]
            passed = parts_ref[0, block, owned:, :]
            for slab in range(1, slabs):
                color = color + passed * parts_ref[slab, block, :owned, :]
                passed = passed * parts_ref[slab, block, owned:, :]
            ends.append((color, passed))
        (color_low, passed_low), (color_high, passed_high) = ends
        red = jnp.where(low, color_low, swapped(color_high))
        green = jnp.where(low, swapped(color_low), color_high)
        opacity = 1.0 - jnp.where(low, passed_low, passed_high)
        at = pair * LANES
        out_ref[:, 0, at : at + LANES] = red
        out_ref[:, 1, at : at + LANES] = green
        out_ref[:, 2, at : at + LANES] = opacity - red
        out_ref[:, 3, at : at + LANES] = opacity


def finish(parts):
    slabs, blocks, rows, _ = parts.shape
    return pl.pallas_call(
        finish_kernel,
        out_shape=jax.ShapeDtypeStruct((rows // 2, 4, blocks * HALF), jnp.float32),
    )(parts)


def shards(samples, tile_list, tile_slot, brick_rank):
    group_count = lax.axis_size("grp")
    swap_count = lax.axis_size("swap")
    slab = lax.axis_index("swap")
    screen = tile_slot.shape[0]
    owned = screen // group_count
    pieces = render(samples[0, 0], group_count)
    arrived = lax.all_to_all(pieces, "grp", split_axis=0, concat_axis=0, tiled=True)
    tiles = lax.dynamic_index_in_dim(tile_list, slab, 0, keepdims=False).reshape(-1)
    ranks = lax.dynamic_index_in_dim(brick_rank, slab, 0, keepdims=False)
    number = jnp.arange(screen, dtype=jnp.int32)
    slots = jnp.sum(
        jnp.where(tiles[None, :] == number[:, None], tile_slot[:, None], 0), axis=0, dtype=jnp.int32
    )
    bricks = jnp.arange(ranks.shape[0], dtype=jnp.int32)
    order = jnp.sum(
        jnp.where(ranks[:, None] == bricks[None, :], bricks[:, None], 0), axis=0, dtype=jnp.int32
    )
    partial_image = composite(arrived, order, slots, owned)
    gathered = lax.all_to_all(partial_image, "grp", split_axis=0, concat_axis=0, tiled=True)
    blocks = group_count // swap_count
    parts = lax.all_to_all(
        gathered.reshape(swap_count, blocks, 2 * owned, LANES),
        "swap",
        split_axis=0,
        concat_axis=0,
        tiled=True,
    )
    return finish(parts)[None]


def solution(mesh):
    return jax.shard_map(
        shards,
        mesh=mesh,
        in_specs=(P("swap", "grp", None, None, None), P(), P(), P()),
        out_specs=P("grp", None, None, "swap"),
        check_vma=False,
    )
```

time: 316 us -> 181 us (0.57)
  waiting for transfers between devices: 199 us -> 69.5 us
  local copies, waits for them, and re-layouts: 56.3 us -> 2.48 us
  blocking collectives: 0 us -> 50.8 us
  Pallas kernels: 0 us -> 43 us
  starting transfers between devices: 30.2 us -> 11.7 us
  other arithmetic: 16.9 us -> 3.14 us
  matrix products: 12.6 us -> 0 us
    all_to_all x1, waiting for transfers between devices: 185 us -> 69.5 us  [shards(): lax.all_to_all(pieces, 'grp', split_axis=0, concat_axis=0, tiled=True)]
    all_to_all x0 -> x2, blocking collectives: none -> 50.8 us  [the longest x1 27.7 us: shards(): lax.all_to_all(gathered.reshape(swap_count, blocks, 2 * owned, LANES), 's...]
    pallas_call x0 -> x3, Pallas kernels: none -> 43 us  [the longest x1 21.6 us: composite(): pl.pallas_call(composite_kernel, in_specs=[pl.BlockSpec(memory_space=pltp...]
    gather x3 -> x0, local copies, waits for them, and re-layouts: 37.4 us -> none  [the longest x2 26 us: slot_tables(): slot_ids = tile_slot[tiles_in]]
    ppermute x3 -> x0, starting transfers between devices: 18.2 us -> none  [from_partner(): lax.ppermute(array, axis, [(i, i ^ 1 << apart) for i in range(lax.axis_si...]
    ppermute x3 -> x0, waiting for transfers between devices: 14.2 us -> none  [from_partner(): lax.ppermute(array, axis, [(i, i ^ 1 << apart) for i in range(lax.axis_si...]
    dot_general x3 -> x0, matrix products: 12.6 us -> none  [the longest x1 8.91 us: combine(): jnp.einsum('of,fcp->ocp', to_rows, shaded, precision=lax.Precision.HIGHEST)]
    select_n x10 -> x0, other arithmetic: 11.5 us -> none  [the longest x2 10.6 us: outgoing(): return jnp.take(padded, source, axis=0)]
  transfers between devices with their start and end apart: 4 -> 1, of which waited for: 4 -> 1; matrix products, arithmetic and copies ran while one was open for 0% -> 2% of each run, Pallas kernels for 0% -> 0%
where the time goes in v1:
time: 181 us
  waiting for transfers between devices  69.5 us (38%)
  blocking collectives  50.8 us (28%)
  Pallas kernels  43 us (24%)
  starting transfers between devices  11.7 us (6%)
  other arithmetic  3.14 us (2%)
  local copies, waits for them, and re-layouts  2.48 us (1%)
    all_to_all x1, waiting for transfers between devices, shards(): lax.all_to_all(pieces, 'grp', split_axis=0, concat_axis=0, tiled=True)  69.5 us
    all_to_all x1, blocking collectives, shards(): lax.all_to_all(gathered.reshape(swap_count, blocks, 2 * owned, LANES), 's...  27.7 us
    all_to_all x1, blocking collectives, shards(): lax.all_to_all(partial_image, 'grp', split_axis=0, concat_axis=0, tiled=T...  23 us
    pallas_call x1, Pallas kernels, composite(): pl.pallas_call(composite_kernel, in_specs=[pl.BlockSpec(memory_space=pltp...  21.6 us
    pallas_call x1, Pallas kernels, render(): pl.pallas_call(render_kernel, grid=(steps,), in_specs=[pl.BlockSpec((frag...  19.6 us
    all_to_all x1, starting transfers between devices, shards(): lax.all_to_all(pieces, 'grp', split_axis=0, concat_axis=0, tiled=True)  11.7 us
  transfers between devices with their start and end apart: 1, of which 1 were waited for; matrix products, arithmetic and copies ran while one was open for 2% of the time, Pallas kernels for 0%

profile of v1, /device:TPU:1, one launch (start us, length us, event | category | flops | bytes accessed | tf_op | source)
XLA Modules:
  0.0 180.6 jit_solution(9095872756298656720)
XLA Ops:
  0.0 0.0 copy-start
  0.0 19.6 %shard_map.46 = f32[64,96,128]{2,1,0:T(8,128)} custom-call(bf16[64,4,4096]{2,1,0:T(4,128)(2,1)} %bitcast.4), custom_call_target="tpu_custom_call" | custom-call | tf_op jit(solution)/shard_map/pallas_call | solution.py:58
  19.6 0.0 copy-start.2
  19.6 11.7 %all-to-all-start = ((f32[64,96,128]{2,1,0:T(8,128)}), f32[64,96,128]{2,1,0:T(8,128)S(1)}, u32[]{:S(2)}, u32[]{:S(2)}) async-start(f32[64,96,128]{2,1,0:T(8,128)} %shard_map.46), calls=%async_computation | async-start | bytes 6291456 | tf_op jit(solution)/shard_map/all_to_all | solution.py:170
  31.4 0.0 copy-done
  31.4 0.1 eq.34
  31.5 0.7 constant_dynamic-slice_fusion.1
  32.2 0.8 select_reduce_fusion.1.order_ref
  33.0 0.0 copy-done.2
  33.0 2.4 %select_reduce_fusion.slots_ref = s32[4096]{0:T(1024)} fusion(s32[512]{0:T(512)S(1)} %copy-done.2, s32[4096]{0:T(1024)S(1)} %eq.34), kind=kLoop, calls=%fused_computation | loop fusion | flops 6287360 | bytes 34816 | tf_op jit(solution)/shard_map/reduce_sum | solution.py:174
  35.4 69.5 %all-to-all-done.pieces_ref = f32[64,96,128]{2,1,0:T(8,128)S(1)} async-done(((f32[64,96,128]{2,1,0:T(8,128)}), f32[64,96,128]{2,1,0:T(8,128)S(1)}, u32[]{:S(2)}, u32[]{:S(2)}) %all-to-all-start) | async-done | bytes 3145760 | tf_op jit(solution)/shard_map/all_to_all | solution.py:170
  104.9 0.0 copy-start.1
  104.9 1.7 copy-done.1
  106.5 21.6 %shard_map.47 = f32[64,16,128]{2,1,0:T(8,128)} custom-call(s32[512]{0:T(512)} %select_reduce_fusion.1.order_ref, s32[4096]{0:T(1024)} %select_reduce_fusion.slots_ref, f32[64,96,128]{2,1,0:T(8,128)} %copy-done.1), custom_call_target="tpu_custom_call" | custom-call | tf_op jit(solution)/shard_map/pallas_call | solution.py:113
  128.1 23.0 %all_to_all.15 = f32[64,16,128]{2,1,0:T(8,128)S(1)} all-to-all(f32[64,16,128]{2,1,0:T(8,128)} %shard_map.47), channel_id=1, replica_groups=mesh['grp'=64,'swap'=8] {'grp'}, dimensions={0} | all-to-all | bytes 1048576 | tf_op jit(solution)/shard_map/all_to_all | solution.py:182
  151.1 27.7 %all_to_all.16.parts_ref = f32[8,8,16,128]{3,2,1,0:T(8,128)} all-to-all(f32[8,8,16,128]{3,2,1,0:T(8,128)S(1)} %bitcast.5), channel_id=1, replica_groups=mesh['grp'=64,'swap'=8] {'swap'}, dimensions={0} | all-to-all | bytes 1048576 | tf_op jit(solution)/shard_map/all_to_all | solution.py:184
  178.9 1.8 shard_map.48
  (1 shorter events, 0.0 us)
Async XLA Ops:
  0.0 31.4 %copy-start = (s32[8,64,64]{2,1,0:T(8,128)S(1)}, s32[8,64,64]{2,1,0:T(8,128)}, u32[]{:S(2)}) copy-start(s32[8,64,64]{2,1,0:T(8,128)} %param.5) | copy-start | bytes 393220
  19.6 13.4 %copy-start.2 = (s32[512]{0:T(512)S(1)}, s32[512]{0:T(512)}, u32[]{:S(2)}) copy-start(s32[512]{0:T(512)} %param.6) | copy-start | bytes 6148
  19.6 85.2 %all-to-all-start = ((f32[64,96,128]{2,1,0:T(8,128)}), f32[64,96,128]{2,1,0:T(8,128)S(1)}, u32[]{:S(2)}, u32[]{:S(2)}) async-start(f32[64,96,128]{2,1,0:T(8,128)} %shard_map.46), calls=%async_computation | async-start | bytes 6291456 | tf_op jit(solution)/shard_map/all_to_all | solution.py:170
  104.9 1.7 copy-start.1

commit v2 on v1

v2 whole, which is shorter than its diff:
```python
import jax
import jax.numpy as jnp
from jax import lax
from jax.experimental import pallas as pl
from jax.experimental.pallas import tpu as pltpu
from jax.sharding import PartitionSpec as P

BRICKS = 8
LANES = 128
HALF = 64

EXTINCTION = 0.024
MESH = pl.DeviceIdType.MESH


def halves(shape):
    return lax.broadcasted_iota(jnp.int32, shape, len(shape) - 1) < HALF


def swapped(value):
    return pltpu.roll(value, HALF, value.ndim - 1)


def chip_at(step, chips):
    columns = 8 if chips % 32 == 0 else 2
    rows = chips // columns
    mine = lax.axis_index("grp") // 2
    turn = columns - 1 - step // rows
    along = ((turn + 1) // 2) * (2 * (turn % 2) - 1)
    x = (mine // columns + step % rows) % rows
    y = (mine % columns + along + columns) % columns
    return x * columns + y


def render_kernel(samples_ref, out_ref, levels, stage, send_sem, recv_sem, own_sem):
    fragments, depth_count, _ = samples_ref.shape
    group_count = out_ref.shape[0]
    chips = group_count // 2
    half = fragments // 2
    early = chips // 4
    me = lax.axis_index("grp")
    slab = lax.axis_index("swap")
    barrier = pltpu.get_barrier_semaphore()

    def greet(step, carry):
        other = (me + step) % group_count
        pl.semaphore_signal(barrier, inc=1, device_id=(other, slab), device_id_type=MESH)
        return carry

    lax.fori_loop(1, group_count, greet, 0)

    def paint(row):
        at = pl.multiple_of(row * LANES, LANES)
        low = halves((fragments, LANES))
        low_half = halves((half, LANES))
        levels[...] = samples_ref[:, :, pl.ds(at, LANES)].astype(jnp.float32)
        passed = jnp.ones((fragments, LANES), jnp.float32)
        red = jnp.zeros((fragments, LANES), jnp.float32)
        green = jnp.zeros((fragments, LANES), jnp.float32)
        for level in range(depth_count):
            value = levels[:, level, :]
            through = jnp.exp(-EXTINCTION * value)
            weight = passed * (1.0 - through)
            rest = 1.0 / (1.0 + value)
            ratio = value * rest
            shade = weight * ratio
            red = red + shade
            green = green + shade * 4.0 * rest
            passed = passed * through
        red_swapped, green_swapped, passed_swapped = swapped(red), swapped(green), swapped(passed)
        stage[2 * row, :fragments, :] = jnp.where(low, red, green_swapped)
        stage[2 * row + 1, :fragments, :] = jnp.where(low, red_swapped, green)
        stage[2 * row, fragments:, :] = jnp.where(low_half, passed[:half], passed_swapped[half:])
        stage[2 * row + 1, fragments:, :] = jnp.where(
            low_half, passed_swapped[:half], passed[half:]
        )

    def sending(target):
        return pltpu.make_async_remote_copy(
            src_ref=stage.at[target],
            dst_ref=out_ref.at[me],
            send_sem=send_sem.at[target],
            recv_sem=recv_sem.at[me],
            device_id=(target, slab),
            device_id_type=MESH,
        )

    def keeping():
        return pltpu.make_async_copy(stage.at[me], out_ref.at[me], own_sem)

    def send(row):
        for side in range(2):
            target = 2 * row + side

            @pl.when(target != me)
            def _():
                sending(target).start()

            @pl.when(target == me)
            def _():
                keeping().start()

    def first(step, carry):
        paint(chip_at(step, chips))
        return carry

    def first_send(step, carry):
        send(chip_at(step, chips))
        return carry

    def later(step, carry):
        row = chip_at(step, chips)
        paint(row)
        send(row)
        return carry

    lax.fori_loop(0, early, first, 0)
    pl.semaphore_wait(barrier, group_count - 1)
    lax.fori_loop(0, early, first_send, 0)
    lax.fori_loop(early, chips, later, 0)

    def finish_one(step, carry):
        other = (me + step) % group_count
        sending(other).wait_send()
        pltpu.make_async_remote_copy(
            src_ref=stage.at[other],
            dst_ref=out_ref.at[other],
            send_sem=send_sem.at[other],
            recv_sem=recv_sem.at[other],
            device_id=(other, slab),
            device_id_type=MESH,
        ).wait_recv()
        return carry

    lax.fori_loop(1, group_count, finish_one, 0)
    keeping().wait()


def render(samples, group_count):
    fragments, depth_count, pixels = samples.shape
    rows = fragments + fragments // 2
    return pl.pallas_call(
        render_kernel,
        in_specs=[pl.BlockSpec(memory_space=pltpu.VMEM)],
        out_specs=pl.BlockSpec(memory_space=pl.ANY),
        out_shape=jax.ShapeDtypeStruct((group_count, rows, LANES), jnp.float32),
        scratch_shapes=[
            pltpu.VMEM((fragments, depth_count, LANES), jnp.float32),
            pltpu.VMEM((group_count, rows, LANES), jnp.float32),
            pltpu.SemaphoreType.DMA((group_count,)),
            pltpu.SemaphoreType.DMA((group_count,)),
            pltpu.SemaphoreType.DMA,
        ],
        compiler_params=pltpu.CompilerParams(collective_id=0, has_side_effects=True),
        cost_estimate=pl.CostEstimate(
            flops=40 * samples.size, bytes_accessed=8 << 20, transcendentals=samples.size
        ),
    )(samples)


def composite_kernel(order_ref, slots_ref, pieces_ref, out_ref, through, colors, passed):
    sources, rows, _ = pieces_ref.shape
    fragments = rows * 2 // 3
    half = fragments // 2
    per_brick = fragments // BRICKS
    low_half = halves((half, LANES))

    def widen(source, carry):
        packed = pieces_ref[source, fragments:, :]
        turned = swapped(packed)
        at = pl.multiple_of(source * fragments, fragments)
        through[pl.ds(at, half), :] = jnp.where(low_half, packed, turned)
        through[pl.ds(at + half, half), :] = jnp.where(low_half, turned, packed)
        return carry

    lax.fori_loop(0, sources, widen, 0)
    colors[...] = jnp.zeros_like(colors)
    passed[...] = jnp.ones_like(passed)

    def brick_step(rank, carry):
        brick = order_ref[rank]
        source = brick // BRICKS
        first = (brick % BRICKS) * per_brick
        number = brick * per_brick
        slots = [slots_ref[number + i] for i in range(per_brick)]
        seen = [passed[pl.ds(slot, 1), :] for slot in slots]
        held = [colors[pl.ds(slot, 1), :] for slot in slots]
        shades = [pieces_ref[source, pl.ds(first + i, 1), :] for i in range(per_brick)]
        fades = [through[pl.ds(number + i, 1), :] for i in range(per_brick)]
        for i in range(per_brick):
            colors[pl.ds(slots[i], 1), :] = held[i] + seen[i] * shades[i]
            passed[pl.ds(slots[i], 1), :] = seen[i] * fades[i]
        return carry

    lax.fori_loop(0, order_ref.shape[0], brick_step, 0)
    groups, packed_rows, _ = out_ref.shape
    size = packed_rows * 2 // 3
    low_size = halves((size // 2, LANES))
    for group in range(groups):
        at = group * size
        middle = at + size // 2
        out_ref[group, :size, :] = colors[at : at + size, :]
        out_ref[group, size:, :] = jnp.where(
            low_size, passed[at:middle, :], passed[middle : at + size, :]
        )


def composite(pieces, order, slots, screen, groups):
    sources, rows, _ = pieces.shape
    fragments = rows * 2 // 3
    size = screen // groups
    return pl.pallas_call(
        composite_kernel,
        in_specs=[
            pl.BlockSpec(memory_space=pltpu.SMEM),
            pl.BlockSpec(memory_space=pltpu.SMEM),
            pl.BlockSpec(memory_space=pltpu.VMEM),
        ],
        out_specs=pl.BlockSpec(memory_space=pltpu.VMEM),
        out_shape=jax.ShapeDtypeStruct((groups, size + size // 2, LANES), jnp.float32),
        scratch_shapes=[
            pltpu.VMEM((sources * fragments, LANES), jnp.float32),
            pltpu.VMEM((screen, LANES), jnp.float32),
            pltpu.VMEM((screen, LANES), jnp.float32),
        ],
    )(order, slots, pieces)


def finish_kernel(
    part_ref, out_ref, arrived, stage, landed, own_sem, send_sem, recv_sem, out_sem, in_sem, here_sem
):
    slabs, packed_rows, _ = part_ref.shape
    size = packed_rows * 2 // 3
    half = size // 2
    blocks, rows, _ = landed.shape
    owned = rows // 2
    me = lax.axis_index("grp")
    slab = lax.axis_index("swap")
    inside = me // blocks == slab
    barrier = pltpu.get_barrier_semaphore()
    for step in range(1, slabs):
        other = (slab + step) % slabs
        pl.semaphore_signal(barrier, inc=1, device_id=(me, other), device_id_type=MESH)
    for block in range(blocks):
        source = slab * blocks + block

        @pl.when(jnp.logical_not(inside & (source == me)))
        def _():
            pl.semaphore_signal(
                barrier, inc=1, device_id=(source, me // blocks), device_id_type=MESH
            )

    own = pltpu.make_async_copy(part_ref.at[slab], arrived.at[slab], own_sem)
    own.start()

    @pl.when(inside)
    def _():
        pl.semaphore_wait(barrier, slabs + blocks - 2)

    @pl.when(jnp.logical_not(inside))
    def _():
        pl.semaphore_wait(barrier, slabs + blocks - 1)

    def across(other):
        return pltpu.make_async_remote_copy(
            src_ref=part_ref.at[other],
            dst_ref=arrived.at[slab],
            send_sem=send_sem.at[other],
            recv_sem=recv_sem.at[slab],
            device_id=(me, other),
            device_id_type=MESH,
        )

    def from_slab(other):
        return pltpu.make_async_remote_copy(
            src_ref=part_ref.at[other],
            dst_ref=arrived.at[other],
            send_sem=send_sem.at[other],
            recv_sem=recv_sem.at[other],
            device_id=(me, other),
            device_id_type=MESH,
        )

    for step in range(1, slabs):
        across((slab + slabs - step) % slabs).start()
    own.wait()
    low_half = halves((half, LANES))
    color = jnp.zeros((size, LANES), jnp.float32)
    passed = [jnp.ones((half, LANES), jnp.float32)] * 2
    for number in range(slabs):

        @pl.when(slab != number)
        def _():
            from_slab(number).wait_recv()

        packed = arrived[number, size:, :]
        turned = swapped(packed)
        color = color + jnp.concatenate(passed, axis=0) * arrived[number, :size, :]
        passed = [
            passed[0] * jnp.where(low_half, packed, turned),
            passed[1] * jnp.where(low_half, turned, packed),
        ]
    passed = jnp.concatenate(passed, axis=0)

    def to_owner(block):
        return pltpu.make_async_remote_copy(
            src_ref=stage.at[block],
            dst_ref=landed.at[me % blocks],
            send_sem=out_sem.at[block],
            recv_sem=in_sem.at[me % blocks],
            device_id=(slab * blocks + block, me // blocks),
            device_id_type=MESH,
        )

    def from_block(block):
        return pltpu.make_async_remote_copy(
            src_ref=stage.at[block],
            dst_ref=landed.at[block],
            send_sem=out_sem.at[block],
            recv_sem=in_sem.at[block],
            device_id=(slab * blocks + block, me // blocks),
            device_id_type=MESH,
        )

    def stay():
        return pltpu.make_async_copy(stage.at[me % blocks], landed.at[me % blocks], here_sem)

    for block in range(blocks):
        stage[block, :owned, :] = color[block * owned : (block + 1) * owned]
        stage[block, owned:, :] = passed[block * owned : (block + 1) * owned]
    for block in range(blocks):
        here = inside & (slab * blocks + block == me)

        @pl.when(here)
        def _():
            stay().start()

        @pl.when(jnp.logical_not(here))
        def _():
            to_owner(block).start()

    for step in range(1, slabs):
        across((slab + slabs - step) % slabs).wait_send()
    for block in range(blocks):
        here = inside & (slab * blocks + block == me)

        @pl.when(here)
        def _():
            stay().wait()

        @pl.when(jnp.logical_not(here))
        def _():
            to_owner(block).wait_send()
            from_block(block).wait_recv()

    low = halves((owned, LANES))
    for pair in range(blocks // 2):
        color_low, passed_low = landed[2 * pair, :owned, :], landed[2 * pair, owned:, :]
        color_high, passed_high = landed[2 * pair + 1, :owned, :], landed[2 * pair + 1, owned:, :]
        red = jnp.where(low, color_low, swapped(color_high))
        green = jnp.where(low, swapped(color_low), color_high)
        opacity = 1.0 - jnp.where(low, passed_low, passed_high)
        at = pair * LANES
        out_ref[:, 0, at : at + LANES] = red
        out_ref[:, 1, at : at + LANES] = green
        out_ref[:, 2, at : at + LANES] = opacity - red
        out_ref[:, 3, at : at + LANES] = opacity


def finish(parts, group_count, owned):
    slabs = parts.shape[0]
    blocks = group_count // slabs
    return pl.pallas_call(
        finish_kernel,
        in_specs=[pl.BlockSpec(memory_space=pltpu.VMEM)],
        out_specs=pl.BlockSpec(memory_space=pltpu.VMEM),
        out_shape=jax.ShapeDtypeStruct((owned, 4, blocks * HALF), jnp.float32),
        scratch_shapes=[
            pltpu.VMEM(parts.shape, jnp.float32),
            pltpu.VMEM((blocks, 2 * owned, LANES), jnp.float32),
            pltpu.VMEM((blocks, 2 * owned, LANES), jnp.float32),
            pltpu.SemaphoreType.DMA,
            pltpu.SemaphoreType.DMA((slabs,)),
            pltpu.SemaphoreType.DMA((slabs,)),
            pltpu.SemaphoreType.DMA((blocks,)),
            pltpu.SemaphoreType.DMA((blocks,)),
            pltpu.SemaphoreType.DMA,
        ],
        compiler_params=pltpu.CompilerParams(collective_id=1, has_side_effects=True),
    )(parts)


def shards(samples, tile_list, tile_slot, brick_rank):
    group_count = lax.axis_size("grp")
    swap_count = lax.axis_size("swap")
    slab = lax.axis_index("swap")
    screen = tile_slot.shape[0]
    owned = screen // group_count
    arrived = render(samples[0, 0], group_count)
    tiles = lax.dynamic_index_in_dim(tile_list, slab, 0, keepdims=False).reshape(-1)
    ranks = lax.dynamic_index_in_dim(brick_rank, slab, 0, keepdims=False)
    number = jnp.arange(screen, dtype=jnp.int32)
    slots = jnp.sum(
        jnp.where(tiles[None, :] == number[:, None], tile_slot[:, None], 0), axis=0, dtype=jnp.int32
    )
    bricks = jnp.arange(ranks.shape[0], dtype=jnp.int32)
    order = jnp.sum(
        jnp.where(ranks[:, None] == bricks[None, :], bricks[:, None], 0), axis=0, dtype=jnp.int32
    )
    parts = composite(arrived, order, slots, screen, swap_count)
    return finish(parts, group_count, owned)[None]


def solution(mesh):
    return jax.shard_map(
        shards,
        mesh=mesh,
        in_specs=(P("swap", "grp", None, None, None), P(), P(), P()),
        out_specs=P("grp", None, None, "swap"),
        check_vma=False,
    )
```

time: 181 us -> 144 us (0.80)
  the two profiles are of different devices: /device:TPU:1 before, /device:TPU:77 now
where the time goes in v2:
time: 144 us
  Pallas kernels  138 us (96%)
  other arithmetic  3.83 us (3%)
  local copies, waits for them, and re-layouts  2.32 us (2%)
    pallas_call x1, Pallas kernels, render(): pl.pallas_call(render_kernel, in_specs=[pl.BlockSpec(memory_space=pltpu.V...  84.1 us
    pallas_call x1, Pallas kernels, finish(): pl.pallas_call(finish_kernel, in_specs=[pl.BlockSpec(memory_space=pltpu.V...  32.1 us
    pallas_call x1, Pallas kernels, composite(): pl.pallas_call(composite_kernel, in_specs=[pl.BlockSpec(memory_space=pltp...  21.5 us
    reduce_sum x1, other arithmetic, shards(): jnp.sum(jnp.where(tiles[None, :] == number[:, None], tile_slot[:, None],...  3.04 us

profile of v2, /device:TPU:77, one launch (start us, length us, event | category | flops | bytes accessed | tf_op | source)
XLA Modules:
  0.0 143.9 jit_solution(11478579271522352313)
XLA Ops:
  0.0 0.0 copy-start
  0.0 0.8 constant_dynamic-slice_fusion.1
  0.8 0.8 select_reduce_fusion.1.order_ref
  1.6 0.0 copy-done
  1.6 0.1 eq.34
  1.6 3.0 %select_reduce_fusion.slots_ref = s32[4096]{0:T(1024)} fusion(s32[512]{0:T(512)} %param.6, s32[4096]{0:T(1024)S(1)} %eq.34), kind=kLoop, calls=%fused_computation | loop fusion | flops 6287360 | bytes 34816 | tf_op jit(solution)/shard_map/reduce_sum | solution.py:403
  4.7 84.1 %shard_map.46.pieces_ref = f32[64,96,128]{2,1,0:T(8,128)} custom-call(bf16[64,4,4096]{2,1,0:T(4,128)(2,1)} %bitcast.3), custom_call_target="tpu_custom_call" | custom-call | flops 41943040 | bytes 8388608 | tf_op jit(solution)/shard_map/pallas_call | solution.py:142
  88.8 21.5 %shard_map.47.part_ref = f32[8,96,128]{2,1,0:T(8,128)} custom-call(s32[512]{0:T(512)} %select_reduce_fusion.1.order_ref, s32[4096]{0:T(1024)} %select_reduce_fusion.slots_ref, f32[64,96,128]{2,1,0:T(8,128)} %shard_map.46.pieces_ref), custom_call_target="tpu_custom_call" | custom-call | tf_op jit(solution)/shard_map/pallas_call | solution.py:212
  110.3 32.1 %shard_map.48 = f32[8,4,512]{2,1,0:T(4,128)} custom-call(f32[8,96,128]{2,1,0:T(8,128)} %shard_map.47.part_ref), custom_call_target="tpu_custom_call" | custom-call | tf_op jit(solution)/shard_map/pallas_call | solution.py:373
  142.4 1.5 %copy.6 = f32[1,8,4,512]{3,2,1,0:T(4,128)} copy(f32[1,8,4,512]{3,2,1,0:T(4,128)} %bitcast.4) | data formatting | bytes 131072
  (1 shorter events, 0.0 us)
Async XLA Ops:
  0.0 1.6 %copy-start = (s32[8,64,64]{2,1,0:T(8,128)S(1)}, s32[8,64,64]{2,1,0:T(8,128)}, u32[]{:S(2)}) copy-start(s32[8,64,64]{2,1,0:T(8,128)} %param.5) | copy-start | bytes 393220

commit v3 on v2

--- a/solution.py
+++ b/solution.py
@@ -1,3 +1,5 @@
+import functools
+
 import jax
 import jax.numpy as jnp
 from jax import lax
@@ -32,7 +34,20 @@
     return x * columns + y
 
 
-def render_kernel(samples_ref, out_ref, levels, stage, send_sem, recv_sem, own_sem):
+def render_kernel(
+    samples_ref,
+    tiles_ref,
+    tile_slot_ref,
+    rank_ref,
+    out_ref,
+    slots_ref,
+    order_ref,
+    levels,
+    stage,
+    send_sem,
+    recv_sem,
+    own_sem,
+):
     fragments, depth_count, _ = samples_ref.shape
     group_count = out_ref.shape[0]
     chips = group_count // 2
@@ -119,6 +134,24 @@
     lax.fori_loop(0, early, first_send, 0)
     lax.fori_loop(early, chips, later, 0)
 
+    tiles = tiles_ref[slab]
+
+    def find_slot(tile, slots):
+        return jnp.where(tiles == tile, tile_slot_ref[tile], slots)
+
+    slots_ref[...] = lax.fori_loop(
+        0, tile_slot_ref.shape[0], find_slot, jnp.zeros_like(tiles), unroll=8
+    )
+    place = lax.broadcasted_iota(jnp.int32, order_ref.shape, 0) * order_ref.shape[1]
+    place = place + lax.broadcasted_iota(jnp.int32, order_ref.shape, 1)
+
+    def find_brick(brick, order):
+        return jnp.where(place == rank_ref[slab, brick], brick, order)
+
+    order_ref[...] = lax.fori_loop(
+        0, rank_ref.shape[1], find_brick, jnp.zeros_like(place), unroll=8
+    )
+
     def finish_one(step, carry):
         other = (me + step) % group_count
         sending(other).wait_send()
@@ -136,14 +169,29 @@
     keeping().wait()
 
 
-def render(samples, group_count):
+def render(samples, tile_list, tile_slot, brick_rank, group_count):
     fragments, depth_count, pixels = samples.shape
     rows = fragments + fragments // 2
+    bricks = brick_rank.shape[1]
+    lanes = min(bricks, LANES)
     return pl.pallas_call(
         render_kernel,
-        in_specs=[pl.BlockSpec(memory_space=pltpu.VMEM)],
-        out_specs=pl.BlockSpec(memory_space=pl.ANY),
-        out_shape=jax.ShapeDtypeStruct((group_count, rows, LANES), jnp.float32),
+        in_specs=[
+            pl.BlockSpec(memory_space=pltpu.VMEM),
+            pl.BlockSpec(memory_space=pltpu.VMEM),
+            pl.BlockSpec(memory_space=pltpu.SMEM),
+            pl.BlockSpec(memory_space=pltpu.SMEM),
+        ],
+        out_specs=(
+            pl.BlockSpec(memory_space=pl.ANY),
+            pl.BlockSpec(memory_space=pltpu.VMEM),
+            pl.BlockSpec(memory_space=pltpu.VMEM),
+        ),
+        out_shape=(
+            jax.ShapeDtypeStruct((group_count, rows, LANES), jnp.float32),
+            jax.ShapeDtypeStruct(tile_list.shape[1:], jnp.int32),
+            jax.ShapeDtypeStruct((bricks // lanes, lanes), jnp.int32),
+        ),
         scratch_shapes=[
             pltpu.VMEM((fragments, depth_count, LANES), jnp.float32),
             pltpu.VMEM((group_count, rows, LANES), jnp.float32),
@@ -155,44 +203,57 @@
         cost_estimate=pl.CostEstimate(
             flops=40 * samples.size, bytes_accessed=8 << 20, transcendentals=samples.size
         ),
-    )(samples)
-
-
-def composite_kernel(order_ref, slots_ref, pieces_ref, out_ref, through, colors, passed):
-    sources, rows, _ = pieces_ref.shape
-    fragments = rows * 2 // 3
+    )(samples, tile_list, tile_slot, brick_rank)
+
+
+def composite_kernel(
+    order_ref, slots_ref, pieces_ref, out_ref, through, colors, passed, *, fragments
+):
+    rows = fragments * 3 // 2
+    sources = pieces_ref.shape[0] // rows
     half = fragments // 2
     per_brick = fragments // BRICKS
+    bricks = sources * BRICKS
+    clear = colors.shape[0] // sources
     low_half = halves((half, LANES))
 
     def widen(source, carry):
-        packed = pieces_ref[source, fragments:, :]
+        start = pl.multiple_of(source * rows + fragments, 8)
+        packed = pieces_ref[pl.ds(start, half), :]
         turned = swapped(packed)
         at = pl.multiple_of(source * fragments, fragments)
         through[pl.ds(at, half), :] = jnp.where(low_half, packed, turned)
         through[pl.ds(at + half, half), :] = jnp.where(low_half, turned, packed)
+        empty = pl.multiple_of(source * clear, clear)
+        colors[pl.ds(empty, clear), :] = jnp.zeros((clear, LANES), jnp.float32)
+        passed[pl.ds(empty, clear), :] = jnp.ones((clear, LANES), jnp.float32)
         return carry
 
     lax.fori_loop(0, sources, widen, 0)
-    colors[...] = jnp.zeros_like(colors)
-    passed[...] = jnp.ones_like(passed)
+
+    def fetch(brick):
+        return tuple(slots_ref[brick * per_brick + i] for i in range(per_brick))
 
     def brick_step(rank, carry):
-        brick = order_ref[rank]
-        source = brick // BRICKS
-        first = (brick % BRICKS) * per_brick
+        brick, after, slots = carry
+        later = order_ref[jnp.minimum(rank + 2, bricks - 1)]
+        slots_after = fetch(after)
+        source = jnp.right_shift(brick, BRICKS.bit_length() - 1)
+        first = source * rows + (brick & (BRICKS - 1)) * per_brick
         number = brick * per_brick
-        slots = [slots_ref[number + i] for i in range(per_brick)]
         seen = [passed[pl.ds(slot, 1), :] for slot in slots]
         held = [colors[pl.ds(slot, 1), :] for slot in slots]
-        shades = [pieces_ref[source, pl.ds(first + i, 1), :] for i in range(per_brick)]
+        shades = [pieces_ref[pl.ds(first + i, 1), :] for i in range(per_brick)]
         fades = [through[pl.ds(number + i, 1), :] for i in range(per_brick)]
         for i in range(per_brick):
+            passed[pl.ds(slots[i], 1), :] = seen[i] * fades[i]
             colors[pl.ds(slots[i], 1), :] = held[i] + seen[i] * shades[i]
-            passed[pl.ds(slots[i], 1), :] = seen[i] * fades[i]
-        return carry
-
-    lax.fori_loop(0, order_ref.shape[0], brick_step, 0)
+        return after, later, slots_after
+
+    first_brick = order_ref[0]
+    lax.fori_loop(
+        0, bricks, brick_step, (first_brick, order_ref[1], fetch(first_brick)), unroll=2
+    )
     groups, packed_rows, _ = out_ref.shape
     size = packed_rows * 2 // 3
     low_size = halves((size // 2, LANES))
@@ -210,7 +271,7 @@
     fragments = rows * 2 // 3
     size = screen // groups
     return pl.pallas_call(
-        composite_kernel,
+        functools.partial(composite_kernel, fragments=fragments),
         in_specs=[
             pl.BlockSpec(memory_space=pltpu.SMEM),
             pl.BlockSpec(memory_space=pltpu.SMEM),
@@ -223,7 +284,7 @@
             pltpu.VMEM((screen, LANES), jnp.float32),
             pltpu.VMEM((screen, LANES), jnp.float32),
         ],
-    )(order, slots, pieces)
+    )(order, slots, pieces.reshape(sources * rows, LANES))
 
 
 def finish_kernel(
@@ -393,21 +454,10 @@
 def shards(samples, tile_list, tile_slot, brick_rank):
     group_count = lax.axis_size("grp")
     swap_count = lax.axis_size("swap")
-    slab = lax.axis_index("swap")
     screen = tile_slot.shape[0]
     owned = screen // group_count
-    arrived = render(samples[0, 0], group_count)
-    tiles = lax.dynamic_index_in_dim(tile_list, slab, 0, keepdims=False).reshape(-1)
-    ranks = lax.dynamic_index_in_dim(brick_rank, slab, 0, keepdims=False)
-    number = jnp.arange(screen, dtype=jnp.int32)
-    slots = jnp.sum(
-        jnp.where(tiles[None, :] == number[:, None], tile_slot[:, None], 0), axis=0, dtype=jnp.int32
-    )
-    bricks = jnp.arange(ranks.shape[0], dtype=jnp.int32)
-    order = jnp.sum(
-        jnp.where(ranks[:, None] == bricks[None, :], bricks[:, None], 0), axis=0, dtype=jnp.int32
-    )
-    parts = composite(arrived, order, slots, screen, swap_count)
+    arrived, slots, order = render(samples[0, 0], tile_list, tile_slot, brick_rank, group_count)
+    parts = composite(arrived, order.reshape(-1), slots.reshape(-1), screen, swap_count)
     return finish(parts, group_count, owned)[None]
 
 

time: 144 us -> 138 us (0.958)
  other arithmetic: 3.83 us -> 0 us
  Pallas kernels: 138 us -> 135 us
    reduce_sum x2 -> x0, other arithmetic: 3.83 us -> none  [the longest x1 3.04 us: shards(): jnp.sum(jnp.where(tiles[None, :] == number[:, None], tile_slot[:, None],...]
    pallas_call x1, Pallas kernels: 21.5 us -> 18 us  [composite(): pl.pallas_call(functools.partial(composite_kernel, fragments=fragments),...]
where the time goes in v3:
time: 138 us
  Pallas kernels  135 us (98%)
  local copies, waits for them, and re-layouts  2.91 us (2%)
    pallas_call x1, Pallas kernels, render(): pl.pallas_call(render_kernel, in_specs=[pl.BlockSpec(memory_space=pltpu.V...  85.1 us
    pallas_call x1, Pallas kernels, finish(): pl.pallas_call(finish_kernel, in_specs=[pl.BlockSpec(memory_space=pltpu.V...  32 us
    pallas_call x1, Pallas kernels, composite(): pl.pallas_call(functools.partial(composite_kernel, fragments=fragments),...  18 us

profile of v3, /device:TPU:77, one launch (start us, length us, event | category | flops | bytes accessed | tf_op | source)
XLA Modules:
  0.0 138.0 jit_solution(6268229014120018095)
XLA Ops:
  0.0 85.1 %shard_map.46 = (f32[64,96,128]{2,1,0:T(8,128)}, s32[64,64]{1,0:T(8,128)}, s32[4,128]{1,0:T(4,128)}) custom-call(bf16[64,4,4096]{2,1,0:T(4,128)(2,1)} %bitcast.5, s32[8,64,64]{2,1,0:T(8,128)} %tiles_ref.1, s32[512]{0:T(512)} %tile_slot_ref.1, s32[8,512]{1,0:T(8,128)} %rank_ref.1), custom_call_target="tpu_custom_call" | custom-call | flops 41943040 | bytes 8388608 | tf_op jit(solution)/shard_map/pallas_call | solution.py:177
  85.1 1.4 %reshape.10.slots_ref = s32[4096]{0:T(1024)} reshape(s32[64,64]{1,0:T(8,128)} %get-tuple-element.9) | data formatting | bytes 32768 | tf_op jit(solution)/shard_map/reshape | solution.py:460
  86.5 18.0 %shard_map.47.part_ref = f32[8,96,128]{2,1,0:T(8,128)} custom-call(s32[512]{0:T(512)} %bitcast.7, s32[4096]{0:T(1024)} %reshape.10.slots_ref, f32[6144,128]{1,0:T(8,128)} %bitcast.4), custom_call_target="tpu_custom_call" | custom-call | tf_op jit(solution)/shard_map/pallas_call | solution.py:273
  104.5 32.0 %shard_map.48 = f32[8,4,512]{2,1,0:T(4,128)} custom-call(f32[8,96,128]{2,1,0:T(8,128)} %shard_map.47.part_ref), custom_call_target="tpu_custom_call" | custom-call | tf_op jit(solution)/shard_map/pallas_call | solution.py:434
  136.5 1.5 %copy.6 = f32[1,8,4,512]{3,2,1,0:T(4,128)} copy(f32[1,8,4,512]{3,2,1,0:T(4,128)} %bitcast.6) | data formatting | bytes 131072

commit v4 on v3

--- a/solution.py
+++ b/solution.py
@@ -42,6 +42,7 @@
     out_ref,
     slots_ref,
     order_ref,
+    start_ref,
     levels,
     stage,
     send_sem,
@@ -52,7 +53,7 @@
     group_count = out_ref.shape[0]
     chips = group_count // 2
     half = fragments // 2
-    early = chips // 4
+    early = chips // 8 if chips % 8 == 0 else 1
     me = lax.axis_index("grp")
     slab = lax.axis_index("swap")
     barrier = pltpu.get_barrier_semaphore()
@@ -137,19 +138,28 @@
     tiles = tiles_ref[slab]
 
     def find_slot(tile, slots):
-        return jnp.where(tiles == tile, tile_slot_ref[tile], slots)
-
-    slots_ref[...] = lax.fori_loop(
+        return jnp.where(tiles == tile, 2 * tile_slot_ref[tile], slots)
+
+    slots = lax.fori_loop(
         0, tile_slot_ref.shape[0], find_slot, jnp.zeros_like(tiles), unroll=8
     )
+    pairs = group_count // 2
+    slots_ref[...] = jnp.concatenate([slots[:pairs], slots[pairs:]], axis=1)
     place = lax.broadcasted_iota(jnp.int32, order_ref.shape, 0) * order_ref.shape[1]
     place = place + lax.broadcasted_iota(jnp.int32, order_ref.shape, 1)
 
     def find_brick(brick, order):
         return jnp.where(place == rank_ref[slab, brick], brick, order)
 
-    order_ref[...] = lax.fori_loop(
-        0, rank_ref.shape[1], find_brick, jnp.zeros_like(place), unroll=8
+    order = lax.fori_loop(0, rank_ref.shape[1], find_brick, jnp.zeros_like(place), unroll=8)
+    per_brick = fragments // BRICKS
+    source = order // BRICKS
+    upper = (source >= pairs).astype(jnp.int32)
+    order_ref[...] = order * (2 * per_brick)
+    start_ref[...] = (
+        (source - upper * pairs) * (2 * fragments)
+        + upper * fragments
+        + (order - source * BRICKS) * per_brick
     )
 
     def finish_one(step, carry):
@@ -186,10 +196,12 @@
             pl.BlockSpec(memory_space=pl.ANY),
             pl.BlockSpec(memory_space=pltpu.VMEM),
             pl.BlockSpec(memory_space=pltpu.VMEM),
+            pl.BlockSpec(memory_space=pltpu.VMEM),
         ),
         out_shape=(
             jax.ShapeDtypeStruct((group_count, rows, LANES), jnp.float32),
-            jax.ShapeDtypeStruct(tile_list.shape[1:], jnp.int32),
+            jax.ShapeDtypeStruct((group_count // 2, 2 * fragments), jnp.int32),
+            jax.ShapeDtypeStruct((bricks // lanes, lanes), jnp.int32),
             jax.ShapeDtypeStruct((bricks // lanes, lanes), jnp.int32),
         ),
         scratch_shapes=[
@@ -207,66 +219,61 @@
 
 
 def composite_kernel(
-    order_ref, slots_ref, pieces_ref, out_ref, through, colors, passed, *, fragments
+    order_ref, start_ref, slots_ref, pieces_ref, out_ref, parts, state, *, fragments
 ):
     rows = fragments * 3 // 2
     sources = pieces_ref.shape[0] // rows
     half = fragments // 2
     per_brick = fragments // BRICKS
     bricks = sources * BRICKS
-    clear = colors.shape[0] // sources
+    clear = state.shape[0] // sources
     low_half = halves((half, LANES))
+    odd = lax.broadcasted_iota(jnp.int32, (clear, LANES), 0) & 1
+    upper = lax.broadcasted_iota(jnp.int32, (2, LANES), 0) == 0
 
     def widen(source, carry):
-        start = pl.multiple_of(source * rows + fragments, 8)
-        packed = pieces_ref[pl.ds(start, half), :]
+        start = pl.multiple_of(source * rows, 8)
+        packed = pieces_ref[pl.ds(start + fragments, half), :]
         turned = swapped(packed)
-        at = pl.multiple_of(source * fragments, fragments)
-        through[pl.ds(at, half), :] = jnp.where(low_half, packed, turned)
-        through[pl.ds(at + half, half), :] = jnp.where(low_half, turned, packed)
-        empty = pl.multiple_of(source * clear, clear)
-        colors[pl.ds(empty, clear), :] = jnp.zeros((clear, LANES), jnp.float32)
-        passed[pl.ds(empty, clear), :] = jnp.ones((clear, LANES), jnp.float32)
+        at = pl.multiple_of(source * (2 * fragments), 8)
+        parts[pl.ds(at, fragments, stride=2), :] = pieces_ref[pl.ds(start, fragments), :]
+        parts[pl.ds(at + 1, half, stride=2), :] = jnp.where(low_half, packed, turned)
+        parts[pl.ds(at + fragments + 1, half, stride=2), :] = jnp.where(low_half, turned, packed)
+        state[pl.ds(pl.multiple_of(source * clear, clear), clear), :] = odd.astype(jnp.float32)
         return carry
 
     lax.fori_loop(0, sources, widen, 0)
 
-    def fetch(brick):
-        return tuple(slots_ref[brick * per_brick + i] for i in range(per_brick))
-
-    def brick_step(rank, carry):
-        brick, after, slots = carry
-        later = order_ref[jnp.minimum(rank + 2, bricks - 1)]
-        slots_after = fetch(after)
-        source = jnp.right_shift(brick, BRICKS.bit_length() - 1)
-        first = source * rows + (brick & (BRICKS - 1)) * per_brick
-        number = brick * per_brick
-        seen = [passed[pl.ds(slot, 1), :] for slot in slots]
-        held = [colors[pl.ds(slot, 1), :] for slot in slots]
-        shades = [pieces_ref[pl.ds(first + i, 1), :] for i in range(per_brick)]
-        fades = [through[pl.ds(number + i, 1), :] for i in range(per_brick)]
+    def fetch(start):
+        return tuple(slots_ref[start + i] for i in range(per_brick))
+
+    def brick_step(rank, slots):
+        slots_after = fetch(start_ref[jnp.minimum(rank + 1, bricks - 1)])
+        at = pl.multiple_of(order_ref[rank], 2 * per_brick)
+        held = [state[pl.ds(pl.multiple_of(slot, 2), 2), :] for slot in slots]
         for i in range(per_brick):
-            passed[pl.ds(slots[i], 1), :] = seen[i] * fades[i]
-            colors[pl.ds(slots[i], 1), :] = held[i] + seen[i] * shades[i]
-        return after, later, slots_after
-
-    first_brick = order_ref[0]
-    lax.fori_loop(
-        0, bricks, brick_step, (first_brick, order_ref[1], fetch(first_brick)), unroll=2
-    )
+            seen = jnp.broadcast_to(held[i][1:], (2, LANES))
+            added = seen * parts[pl.ds(at + 2 * i, 2), :]
+            state[pl.ds(pl.multiple_of(slots[i], 2), 2), :] = added + jnp.where(
+                upper, held[i], 0.0
+            )
+        return slots_after
+
+    lax.fori_loop(0, bricks, brick_step, fetch(start_ref[0]), unroll=2)
     groups, packed_rows, _ = out_ref.shape
     size = packed_rows * 2 // 3
     low_size = halves((size // 2, LANES))
     for group in range(groups):
-        at = group * size
-        middle = at + size // 2
-        out_ref[group, :size, :] = colors[at : at + size, :]
+        at = group * 2 * size
+        out_ref[group, :size, :] = state[pl.ds(at, size, stride=2), :]
         out_ref[group, size:, :] = jnp.where(
-            low_size, passed[at:middle, :], passed[middle : at + size, :]
-        )
-
-
-def composite(pieces, order, slots, screen, groups):
+            low_size,
+            state[pl.ds(at + 1, size // 2, stride=2), :],
+            state[pl.ds(at + size + 1, size // 2, stride=2), :],
+        )
+
+
+def composite(pieces, order, start, slots, screen, groups):
     sources, rows, _ = pieces.shape
     fragments = rows * 2 // 3
     size = screen // groups
@@ -275,22 +282,23 @@
         in_specs=[
             pl.BlockSpec(memory_space=pltpu.SMEM),
             pl.BlockSpec(memory_space=pltpu.SMEM),
+            pl.BlockSpec(memory_space=pltpu.SMEM),
             pl.BlockSpec(memory_space=pltpu.VMEM),
         ],
         out_specs=pl.BlockSpec(memory_space=pltpu.VMEM),
         out_shape=jax.ShapeDtypeStruct((groups, size + size // 2, LANES), jnp.float32),
         scratch_shapes=[
-            pltpu.VMEM((sources * fragments, LANES), jnp.float32),
-            pltpu.VMEM((screen, LANES), jnp.float32),
-            pltpu.VMEM((screen, LANES), jnp.float32),
+            pltpu.VMEM((2 * sources * fragments, LANES), jnp.float32),
+            pltpu.VMEM((2 * screen, LANES), jnp.float32),
         ],
-    )(order, slots, pieces.reshape(sources * rows, LANES))
+    )(order, start, slots, pieces.reshape(sources * rows, LANES))
 
 
 def finish_kernel(
     part_ref, out_ref, arrived, stage, landed, own_sem, send_sem, recv_sem, out_sem, in_sem, here_sem
 ):
-    slabs, packed_rows, _ = part_ref.shape
+    packed_rows = part_ref.shape[1]
+    slabs = part_ref.shape[0] // 2
     size = packed_rows * 2 // 3
     half = size // 2
     blocks, rows, _ = landed.shape
@@ -311,8 +319,13 @@
                 barrier, inc=1, device_id=(source, me // blocks), device_id_type=MESH
             )
 
-    own = pltpu.make_async_copy(part_ref.at[slab], arrived.at[slab], own_sem)
-    own.start()
+    def own(side):
+        return pltpu.make_async_copy(
+            part_ref.at[2 * slab + side], arrived.at[side, slab], own_sem.at[side]
+        )
+
+    own(0).start()
+    own(1).start()
 
     @pl.when(inside)
     def _():
@@ -322,46 +335,49 @@
     def _():
         pl.semaphore_wait(barrier, slabs + blocks - 1)
 
-    def across(other):
+    def across(side, other):
         return pltpu.make_async_remote_copy(
-            src_ref=part_ref.at[other],
-            dst_ref=arrived.at[slab],
-            send_sem=send_sem.at[other],
-            recv_sem=recv_sem.at[slab],
+            src_ref=part_ref.at[2 * other + side],
+            dst_ref=arrived.at[side, slab],
+            send_sem=send_sem.at[side, other],
+            recv_sem=recv_sem.at[side, slab],
             device_id=(me, other),
             device_id_type=MESH,
         )
 
-    def from_slab(other):
+    def from_slab(side, other):
         return pltpu.make_async_remote_copy(
-            src_ref=part_ref.at[other],
-            dst_ref=arrived.at[other],
-            send_sem=send_sem.at[other],
-            recv_sem=recv_sem.at[other],
+            src_ref=part_ref.at[2 * other + side],
+            dst_ref=arrived.at[side, other],
+            send_sem=send_sem.at[side, other],
+            recv_sem=recv_sem.at[side, other],
             device_id=(me, other),
             device_id_type=MESH,
         )
 
-    for step in range(1, slabs):
-        across((slab + slabs - step) % slabs).start()
-    own.wait()
+    for side in range(2):
+        for step in range(1, slabs):
+            across(side, (slab + slabs - step) % slabs).start()
     low_half = halves((half, LANES))
-    color = jnp.zeros((size, LANES), jnp.float32)
-    passed = [jnp.ones((half, LANES), jnp.float32)] * 2
-    for number in range(slabs):
-
-        @pl.when(slab != number)
-        def _():
-            from_slab(number).wait_recv()
-
-        packed = arrived[number, size:, :]
-        turned = swapped(packed)
-        color = color + jnp.concatenate(passed, axis=0) * arrived[number, :size, :]
-        passed = [
-            passed[0] * jnp.where(low_half, packed, turned),
-            passed[1] * jnp.where(low_half, turned, packed),
-        ]
-    passed = jnp.concatenate(passed, axis=0)
+
+    def merge(side):
+        own(side).wait()
+        color = jnp.zeros((size, LANES), jnp.float32)
+        passed = [jnp.ones((half, LANES), jnp.float32)] * 2
+        for number in range(slabs):
+
+            @pl.when(slab != number)
+            def _():
+                from_slab(side, number).wait_recv()
+
+            packed = arrived[side, number, size:, :]
+            turned = swapped(packed)
+            color = color + jnp.concatenate(passed, axis=0) * arrived[side, number, :size, :]
+            passed = [
+                passed[0] * jnp.where(low_half, packed, turned),
+                passed[1] * jnp.where(low_half, turned, packed),
+            ]
+        return color, jnp.concatenate(passed, axis=0)
 
     def to_owner(block):
         return pltpu.make_async_remote_copy(
@@ -386,22 +402,27 @@
     def stay():
         return pltpu.make_async_copy(stage.at[me % blocks], landed.at[me % blocks], here_sem)
 
-    for block in range(blocks):
-        stage[block, :owned, :] = color[block * owned : (block + 1) * owned]
-        stage[block, owned:, :] = passed[block * owned : (block + 1) * owned]
-    for block in range(blocks):
-        here = inside & (slab * blocks + block == me)
-
-        @pl.when(here)
-        def _():
-            stay().start()
-
-        @pl.when(jnp.logical_not(here))
-        def _():
-            to_owner(block).start()
-
-    for step in range(1, slabs):
-        across((slab + slabs - step) % slabs).wait_send()
+    for side in range(2):
+        color, passed = merge(side)
+        first = side * blocks // 2
+        for block in range(first, first + blocks // 2):
+            at = (block - first) * owned
+            stage[block, :owned, :] = color[at : at + owned]
+            stage[block, owned:, :] = passed[at : at + owned]
+        for block in range(first, first + blocks // 2):
+            here = inside & (slab * blocks + block == me)
+
+            @pl.when(here)
+            def _():
+                stay().start()
+
+            @pl.when(jnp.logical_not(here))
+            def _():
+                to_owner(block).start()
+
+    for side in range(2):
+        for step in range(1, slabs):
+            across(side, (slab + slabs - step) % slabs).wait_send()
     for block in range(blocks):
         here = inside & (slab * blocks + block == me)
 
@@ -428,8 +449,7 @@
         out_ref[:, 3, at : at + LANES] = opacity
 
 
-def finish(parts, group_count, owned):
-    slabs = parts.shape[0]
+def finish(parts, slabs, group_count, owned):
     blocks = group_count // slabs
     return pl.pallas_call(
         finish_kernel,
@@ -437,12 +457,12 @@
         out_specs=pl.BlockSpec(memory_space=pltpu.VMEM),
         out_shape=jax.ShapeDtypeStruct((owned, 4, blocks * HALF), jnp.float32),
         scratch_shapes=[
-            pltpu.VMEM(parts.shape, jnp.float32),
+            pltpu.VMEM((2, slabs) + parts.shape[1:], jnp.float32),
             pltpu.VMEM((blocks, 2 * owned, LANES), jnp.float32),
             pltpu.VMEM((blocks, 2 * owned, LANES), jnp.float32),
-            pltpu.SemaphoreType.DMA,
-            pltpu.SemaphoreType.DMA((slabs,)),
-            pltpu.SemaphoreType.DMA((slabs,)),
+            pltpu.SemaphoreType.DMA((2,)),
+            pltpu.SemaphoreType.DMA((2, slabs)),
+            pltpu.SemaphoreType.DMA((2, slabs)),
             pltpu.SemaphoreType.DMA((blocks,)),
             pltpu.SemaphoreType.DMA((blocks,)),
             pltpu.SemaphoreType.DMA,
@@ -456,9 +476,13 @@
     swap_count = lax.axis_size("swap")
     screen = tile_slot.shape[0]
     owned = screen // group_count
-    arrived, slots, order = render(samples[0, 0], tile_list, tile_slot, brick_rank, group_count)
-    parts = composite(arrived, order.reshape(-1), slots.reshape(-1), screen, swap_count)
-    return finish(parts, group_count, owned)[None]
+    arrived, slots, order, start = render(
+        samples[0, 0], tile_list, tile_slot, brick_rank, group_count
+    )
+    parts = composite(
+        arrived, order.reshape(-1), start.reshape(-1), slots.reshape(-1), screen, 2 * swap_count
+    )
+    return finish(parts, swap_count, group_count, owned)[None]
 
 
 def solution(mesh):

time: 138 us -> 134 us (0.971)
  the two profiles are of different devices: /device:TPU:77 before, /device:TPU:63 now
where the time goes in v4:
time: 134 us
  Pallas kernels  132 us (99%)
  local copies, waits for them, and re-layouts  1.47 us (1%)
    pallas_call x1, Pallas kernels, render(): pl.pallas_call(render_kernel, in_specs=[pl.BlockSpec(memory_space=pltpu.V...  85.4 us
    pallas_call x1, Pallas kernels, finish(): pl.pallas_call(finish_kernel, in_specs=[pl.BlockSpec(memory_space=pltpu.V...  32.1 us
    pallas_call x1, Pallas kernels, composite(): pl.pallas_call(functools.partial(composite_kernel, fragments=fragments),...  15 us

profile of v4, /device:TPU:63, one launch (start us, length us, event | category | flops | bytes accessed | tf_op | source)
XLA Modules:
  0.0 134.0 jit_solution(7211794769054412586)
XLA Ops:
  0.0 85.4 %shard_map.46 = (f32[64,96,128]{2,1,0:T(8,128)}, s32[32,128]{1,0:T(8,128)}, s32[4,128]{1,0:T(4,128)}, s32[4,128]{1,0:T(4,128)}) custom-call(bf16[64,4,4096]{2,1,0:T(4,128)(2,1)} %bitcast.7, s32[8,64,64]{2,1,0:T(8,128)} %tiles_ref.1, s32[512]{0:T(512)} %tile_slot_ref.1, s32[8,512]{1,0:T(8,128)} %rank_ref.1), custom_call_target="tpu_custom_call" | custom-call | flops 41943040 | bytes 8388608 | tf_op jit(solution)/shard_map/pallas_call | solution.py:187
  85.4 15.0 %shard_map.47.part_ref = f32[16,48,128]{2,1,0:T(8,128)} custom-call(s32[512]{0:T(512)} %bitcast.10, s32[512]{0:T(512)} %bitcast.11, s32[4096]{0:T(1024)} %bitcast.9, f32[6144,128]{1,0:T(8,128)} %bitcast.6), custom_call_target="tpu_custom_call" | custom-call | tf_op jit(solution)/shard_map/pallas_call | solution.py:280
  100.4 32.1 %shard_map.48 = f32[8,4,512]{2,1,0:T(4,128)} custom-call(f32[16,48,128]{2,1,0:T(8,128)} %shard_map.47.part_ref), custom_call_target="tpu_custom_call" | custom-call | tf_op jit(solution)/shard_map/pallas_call | solution.py:454
  132.5 1.5 %copy.6 = f32[1,8,4,512]{3,2,1,0:T(4,128)} copy(f32[1,8,4,512]{3,2,1,0:T(4,128)} %bitcast.8) | data formatting | bytes 131072

commit v5 on v4

--- a/solution.py
+++ b/solution.py
@@ -27,7 +27,7 @@
     columns = 8 if chips % 32 == 0 else 2
     rows = chips // columns
     mine = lax.axis_index("grp") // 2
-    turn = columns - 1 - step // rows
+    turn = columns - 1 - (step // rows + step % rows) % columns
     along = ((turn + 1) // 2) * (2 * (turn % 2) - 1)
     x = (mine // columns + step % rows) % rows
     y = (mine % columns + along + columns) % columns

time: 134 us -> 130 us (0.970)
  the two profiles are of different devices: /device:TPU:63 before, /device:TPU:61 now
where the time goes in v5:
time: 130 us
  Pallas kernels  129 us (99%)
  local copies, waits for them, and re-layouts  1.47 us (1%)
    pallas_call x1, Pallas kernels, render(): pl.pallas_call(render_kernel, in_specs=[pl.BlockSpec(memory_space=pltpu.V...  84 us
    pallas_call x1, Pallas kernels, finish(): pl.pallas_call(finish_kernel, in_specs=[pl.BlockSpec(memory_space=pltpu.V...  29.8 us
    pallas_call x1, Pallas kernels, composite(): pl.pallas_call(functools.partial(composite_kernel, fragments=fragments),...  15 us

profile of v5, /device:TPU:61, one launch (start us, length us, event | category | flops | bytes accessed | tf_op | source)
XLA Modules:
  0.0 130.2 jit_solution(3796363268344444134)
XLA Ops:
  0.0 84.0 %shard_map.46 = (f32[64,96,128]{2,1,0:T(8,128)}, s32[32,128]{1,0:T(8,128)}, s32[4,128]{1,0:T(4,128)}, s32[4,128]{1,0:T(4,128)}) custom-call(bf16[64,4,4096]{2,1,0:T(4,128)(2,1)} %bitcast.7, s32[8,64,64]{2,1,0:T(8,128)} %tiles_ref.1, s32[512]{0:T(512)} %tile_slot_ref.1, s32[8,512]{1,0:T(8,128)} %rank_ref.1), custom_call_target="tpu_custom_call" | custom-call | flops 41943040 | bytes 8388608 | tf_op jit(solution)/shard_map/pallas_call | solution.py:187
  84.0 15.0 %shard_map.47.part_ref = f32[16,48,128]{2,1,0:T(8,128)} custom-call(s32[512]{0:T(512)} %bitcast.10, s32[512]{0:T(512)} %bitcast.11, s32[4096]{0:T(1024)} %bitcast.9, f32[6144,128]{1,0:T(8,128)} %bitcast.6), custom_call_target="tpu_custom_call" | custom-call | tf_op jit(solution)/shard_map/pallas_call | solution.py:280
  98.9 29.8 %shard_map.48 = f32[8,4,512]{2,1,0:T(4,128)} custom-call(f32[16,48,128]{2,1,0:T(8,128)} %shard_map.47.part_ref), custom_call_target="tpu_custom_call" | custom-call | tf_op jit(solution)/shard_map/pallas_call | solution.py:454
  128.7 1.5 %copy.6 = f32[1,8,4,512]{3,2,1,0:T(4,128)} copy(f32[1,8,4,512]{3,2,1,0:T(4,128)} %bitcast.8) | data formatting | bytes 131072
